TPU v7x, 32 devices: a whole 2x2x4 slice. The times are simulated.
32 devices in a mesh: replica: 8 (over y, x, core), shard: 4 (over z).
Axes of the slice: x: 2, y: 2, z: 4, core: 2. Of those that a mesh axis runs over, the one named last changes fastest.
Arguments:
- inputs: bfloat16 [4096, 2048], P(('replica', 'shard')), may hold values from -6 to 6
- lengths: int32 [8, 8], P('replica'), may hold values from 1 to 256, 512 in all within a row
- ln_gain: float32 [2048], replicated, may hold values from 0.5 to 1.5
- ln_bias: float32 [2048], replicated, may hold values from -3 to 3
- qkv_weight: bfloat16 [2048, 3, 2048], P(None, None, 'shard'), may hold values from -0.125 to 0.125
- qkv_bias: float32 [3, 2048], P(None, 'shard'), may hold values from -3 to 3
- out_weight: bfloat16 [2048, 2048], P('shard'), may hold values from -0.5 to 0.5
- fc1_weight: bfloat16 [2048, 8192], P(None, 'shard'), may hold values from -0.125 to 0.125
- fc1_bias: float32 [8192], P('shard'), may hold values from -3 to 3
- fc2_weight: bfloat16 [8192, 2048], P('shard'), may hold values from -0.0625 to 0.0625
- out_bias: float32 [2048], replicated, may hold values from -3 to 3
- cotangent: bfloat16 [4096, 2048], P(('replica', 'shard')), may hold values from -6 to 6
Outputs:
- output: bfloat16 [4096, 2048], P(('replica', 'shard'))
- input_grad: float32 [4096, 2048], P(('replica', 'shard'))
- ln_gain_grad: float32 [2048], P('shard')
- ln_bias_grad: float32 [2048], P('shard')
- qkv_weight_grad: float32 [2048, 3, 2048], P(None, None, 'shard')
- qkv_bias_grad: float32 [3, 2048], P(None, 'shard')
- out_weight_grad: float32 [2048, 2048], P('shard')
- fc1_weight_grad: float32 [2048, 8192], P(None, 'shard')
- fc1_bias_grad: float32 [8192], P('shard')
- fc2_weight_grad: float32 [8192, 2048], P('shard')
- out_bias_grad: float32 [2048], replicated
Inputs may be any that keep to these rules, and one draw needn't show every extreme that they name: Row g of lengths holds the lengths of the 8 sequences of replica group g in order; they add up to 512, and the longest is 256.
All inputs are finite; a program needn't handle non-finite values.
Results may differ from a plain program's by a relative error of at most 0.011.
Values may be sent and summed in bfloat16 or wider, within the bound.
No kernel may reach another device: no remote copies, remote signals or barrier semaphores. Data moves between devices by JAX's collectives and lax.ppermute only.
A program may use at most 320 MiB of HBM per device.

v0:
```python
import math

import jax
import jax.numpy as jnp
from jax import lax
from jax.sharding import PartitionSpec as P

HD = 64
ROT = 32


def normalize(x_float):
    mean_row = jnp.mean(x_float, axis=-1, keepdims=True)
    centred = x_float - mean_row
    inv_std = lax.rsqrt(jnp.mean(centred * centred, axis=-1, keepdims=True) + 1e-05)
    return (centred * inv_std, inv_std)


def positions(length_row, count):
    ends = jnp.cumsum(length_row, dtype=jnp.int32)
    row_ids = jnp.arange(count, dtype=jnp.int32)
    passed = (row_ids[:, None] >= ends[None, :]).astype(jnp.int32)
    segment = jnp.sum(passed, axis=1, dtype=jnp.int32)
    begin = jnp.sum(passed * length_row[None, :], axis=1, dtype=jnp.int32)
    offset = (row_ids - begin).astype(jnp.float32)
    freq_ids = jnp.arange(ROT // 2, dtype=jnp.float32)
    inverse = jnp.exp(freq_ids * (-2.0 * math.log(10000.0) / ROT))
    angle_rows = offset[:, None] * inverse[None, :]
    return (segment, row_ids, jnp.cos(angle_rows), jnp.sin(angle_rows))


def rotate(values, cosine, sine):
    half = ROT // 2
    first = values[..., :half]
    second = values[..., half:ROT]
    cos_b = cosine[:, None, :]
    sin_b = sine[:, None, :]
    return jnp.concatenate(
        [first * cos_b - second * sin_b, second * cos_b + first * sin_b, values[..., ROT:]], axis=-1
    )


def unrotate(values, cosine, sine):
    half = ROT // 2
    first = values[..., :half]
    second = values[..., half:ROT]
    cos_b = cosine[:, None, :]
    sin_b = sine[:, None, :]
    return jnp.concatenate(
        [first * cos_b + second * sin_b, second * cos_b - first * sin_b, values[..., ROT:]], axis=-1
    )


def gelu_tanh(inner):
    coef = math.sqrt(2.0 / math.pi)
    return 0.5 * inner * (1.0 + jnp.tanh(coef * (inner + 0.044715 * inner * inner * inner)))


def gelu_slope(inner):
    coef = math.sqrt(2.0 / math.pi)
    tangent = jnp.tanh(coef * (inner + 0.044715 * inner * inner * inner))
    return 0.5 * (1.0 + tangent) + 0.5 * inner * (1.0 - tangent * tangent) * coef * (
        1.0 + 3.0 * 0.044715 * inner * inner
    )


def allowed_mask(seg_block, row_block, segment, row_ids):
    return (seg_block[:, None] == segment[None, :]) & (row_ids[None, :] <= row_block[:, None])


def attend(query, keys, values, segment, row_ids):
    count, heads = (query.shape[0], query.shape[1])
    block = min(512, count)
    blocks = count // block

    def per_block(entry):
        q_block, seg_block, row_block = entry
        scores = (
            jnp.einsum("qhd,khd->hqk", q_block, keys, preferred_element_type=jnp.float32) * 0.125
        )
        allowed = allowed_mask(seg_block, row_block, segment, row_ids)[None]
        log_total = jnp.log(jnp.sum(jnp.where(allowed, jnp.exp(scores), 0.0), axis=-1))
        probs = jnp.where(allowed, jnp.exp(scores - log_total[..., None]), 0.0).astype(jnp.bfloat16)
        context = jnp.einsum(
            "hqk,khd->qhd", probs, values, preferred_element_type=jnp.float32
        ).astype(jnp.bfloat16)
        return (context, log_total)

    contexts, totals = lax.map(
        per_block,
        (
            query.reshape(blocks, block, heads, HD),
            segment.reshape(blocks, block),
            row_ids.reshape(blocks, block),
        ),
    )
    return (contexts.reshape(count, heads, HD), totals)


def attend_back(query, keys, values, totals, grad_context, segment, row_ids):
    count, heads = (query.shape[0], query.shape[1])
    block = min(512, count)
    blocks = count // block

    def per_block(carry, entry):
        grad_keys, grad_values = carry
        q_block, g_block, total_block, seg_block, row_block = entry
        scores = (
            jnp.einsum("qhd,khd->hqk", q_block, keys, preferred_element_type=jnp.float32) * 0.125
        )
        allowed = allowed_mask(seg_block, row_block, segment, row_ids)[None]
        probs = jnp.where(allowed, jnp.exp(scores - total_block[..., None]), 0.0)
        probs_low = probs.astype(jnp.bfloat16)
        grad_probs = jnp.einsum("qhd,khd->hqk", g_block, values, preferred_element_type=jnp.float32)
        grad_scores = (
            probs * (grad_probs - jnp.sum(probs * grad_probs, axis=-1, keepdims=True)) * 0.125
        ).astype(jnp.bfloat16)
        grad_query = jnp.einsum(
            "hqk,khd->qhd", grad_scores, keys, preferred_element_type=jnp.float32
        )
        grad_keys = grad_keys + jnp.einsum(
            "hqk,qhd->khd", grad_scores, q_block, preferred_element_type=jnp.float32
        )
        grad_values = grad_values + jnp.einsum(
            "hqk,qhd->khd", probs_low, g_block, preferred_element_type=jnp.float32
        )
        return ((grad_keys, grad_values), grad_query)

    zeros = jnp.zeros(keys.shape, jnp.float32)
    stacked = (
        query.reshape(blocks, block, heads, HD),
        grad_context.reshape(blocks, block, heads, HD),
        totals,
        segment.reshape(blocks, block),
        row_ids.reshape(blocks, block),
    )
    (grad_keys, grad_values), grad_queries = lax.scan(per_block, (zeros, zeros), stacked)
    return (grad_queries.reshape(count, heads, HD), grad_keys, grad_values)


def shards(
    inputs,
    lengths,
    ln_gain,
    ln_bias,
    qkv_weight,
    qkv_bias,
    out_weight,
    fc1_weight,
    fc1_bias,
    fc2_weight,
    out_bias,
    cotangent,
):
    rows_dev, width = inputs.shape
    qkv_flat = qkv_weight.reshape(width, -1)
    qkv_cols = qkv_flat.shape[1]
    heads_local = qkv_cols // (3 * HD)
    x_float = inputs.astype(jnp.float32)
    x_hat, inv_std = normalize(x_float)
    normed = (x_hat * ln_gain + ln_bias).astype(jnp.bfloat16)
    normed_full = lax.all_gather(normed, "shard", axis=0, tiled=True)
    qkv_pre = jnp.dot(normed_full, qkv_flat, preferred_element_type=jnp.float32)
    pre = jnp.dot(normed_full, fc1_weight, preferred_element_type=jnp.float32)
    group_rows = qkv_pre.shape[0]
    qkv = (qkv_pre + qkv_bias.reshape(-1)).reshape(group_rows, 3, heads_local, HD)
    segment, row_ids, cosine, sine = positions(lengths[0], group_rows)
    query = rotate(qkv[:, 0], cosine, sine).astype(jnp.bfloat16)
    keys = rotate(qkv[:, 1], cosine, sine).astype(jnp.bfloat16)
    values = qkv[:, 2].astype(jnp.bfloat16)
    context, totals = attend(query, keys, values, segment, row_ids)
    context_flat = context.reshape(group_rows, -1)
    pre = pre + fc1_bias
    hidden = gelu_tanh(pre).astype(jnp.bfloat16)
    mixed = lax.psum_scatter(
        jnp.dot(context_flat, out_weight, preferred_element_type=jnp.float32)
        + jnp.dot(hidden, fc2_weight, preferred_element_type=jnp.float32),
        "shard",
        scatter_dimension=0,
        tiled=True,
    )
    output = (x_float + mixed + out_bias).astype(jnp.bfloat16)
    cot_full = lax.all_gather(cotangent, "shard", axis=0, tiled=True)
    grad_out_w = jnp.dot(context_flat.T, cot_full, preferred_element_type=jnp.float32)
    grad_fc2 = jnp.dot(hidden.T, cot_full, preferred_element_type=jnp.float32)
    grad_out_b = jnp.sum(cot_full, axis=0, dtype=jnp.float32)
    grad_pre = jnp.dot(cot_full, fc2_weight.T, preferred_element_type=jnp.float32) * gelu_slope(pre)
    grad_fc1_b = jnp.sum(grad_pre, axis=0)
    grad_pre_low = grad_pre.astype(jnp.bfloat16)
    grad_fc1 = jnp.dot(normed_full.T, grad_pre_low, preferred_element_type=jnp.float32)
    grad_context = (
        jnp.dot(cot_full, out_weight.T, preferred_element_type=jnp.float32)
        .astype(jnp.bfloat16)
        .reshape(group_rows, heads_local, HD)
    )
    grad_query, grad_keys, grad_values = attend_back(
        query, keys, values, totals, grad_context, segment, row_ids
    )
    grad_qkv = jnp.stack(
        [unrotate(grad_query, cosine, sine), unrotate(grad_keys, cosine, sine), grad_values], axis=1
    ).reshape(group_rows, qkv_cols)
    grad_qkv_b = jnp.sum(grad_qkv, axis=0).reshape(qkv_bias.shape)
    grad_qkv_low = grad_qkv.astype(jnp.bfloat16)
    grad_qkv_w = jnp.dot(normed_full.T, grad_qkv_low, preferred_element_type=jnp.float32).reshape(
        qkv_weight.shape
    )
    grad_normed = lax.psum_scatter(
        jnp.dot(grad_qkv_low, qkv_flat.T, preferred_element_type=jnp.float32)
        + jnp.dot(grad_pre_low, fc1_weight.T, preferred_element_type=jnp.float32),
        "shard",
        scatter_dimension=0,
        tiled=True,
    )
    norm_parts = jnp.stack(
        [jnp.sum(grad_normed * x_hat, axis=0), jnp.sum(grad_normed, axis=0)], axis=0
    )
    norm_shares = lax.psum_scatter(norm_parts, "shard", scatter_dimension=1, tiled=True)
    scaled = grad_normed * ln_gain
    input_grad = cotangent.astype(jnp.float32) + inv_std * (
        scaled
        - jnp.mean(scaled, axis=-1, keepdims=True)
        - x_hat * jnp.mean(scaled * x_hat, axis=-1, keepdims=True)
    )
    grad_qkv_w, grad_qkv_b, grad_out_w, grad_fc1, grad_fc1_b, grad_fc2, grad_out_b, norm_shares = (
        lax.psum(
            (
                grad_qkv_w,
                grad_qkv_b,
                grad_out_w,
                grad_fc1,
                grad_fc1_b,
                grad_fc2,
                grad_out_b,
                norm_shares,
            ),
            "replica",
        )
    )
    return (
        output,
        input_grad,
        norm_shares[0],
        norm_shares[1],
        grad_qkv_w,
        grad_qkv_b,
        grad_out_w,
        grad_fc1,
        grad_fc1_b,
        grad_fc2,
        grad_out_b,
    )


def solution(mesh):
    placed = (
        P(("replica", "shard"), None),
        P("replica", None),
        P(),
        P(),
        P(None, None, "shard"),
        P(None, "shard"),
        P("shard", None),
        P(None, "shard"),
        P("shard"),
        P("shard", None),
        P(),
        P(("replica", "shard"), None),
    )
    return jax.shard_map(
        shards,
        mesh=mesh,
        in_specs=placed,
        out_specs=(
            P(("replica", "shard"), None),
            P(("replica", "shard"), None),
            P("shard"),
            P("shard"),
            P(None, None, "shard"),
            P(None, "shard"),
            P("shard", None),
            P(None, "shard"),
            P("shard"),
            P("shard", None),
            P(),
        ),
        check_vma=False,
    )
```

profile of v0, /device:TPU:0, one launch (start us, length us, event | category | flops | bytes accessed | tf_op | source)
XLA Modules:
  0.0 1005.6 jit_solution(11265789539171059828)
XLA Ops:
  13.7 8.8 copy.45
  23.2 37.5 %all-gather.3.cloned.1.call-done = bf16[512,2048]{1,0:T(8,128)(2,1)} async-done(((bf16[128,2048]{1,0:T(8,128)(2,1)}), bf16[512,2048]{1,0:T(8,128)(2,1)}) %all-gather.3.cloned.1.call-update) | async-done | bytes 2097168 | tf_op jit(solution)/shard_map/all_gather | solution.py:162
  60.7 8.5 convolution_add_fusion.1
  76.5 30.3 %all-gather.5.cloned.1.call-done = bf16[512,2048]{1,0:T(8,128)(2,1)} async-done(((bf16[128,2048]{1,0:T(8,128)(2,1)}), bf16[512,2048]{1,0:T(8,128)(2,1)}) %all-gather.5.cloned.1.call-update) | async-done | bytes 2097168 | tf_op jit(solution)/shard_map/all_gather | solution.py:183
  109.7 6.1 fusion.70
  116.8 8.6 fusion.3
  125.4 5.0 fusion.35
  130.3 14.3 %fusion.38 = f32[512,8,64]{0,2,1:T(8,128)} fusion(f32[8,512,512]{1,2,0:T(8,128)} %fusion.3, f32[8,512,512]{1,2,0:T(8,128)} %fusion.70, bf16[512,8,32]{0,2,1:T(8,128)(2,1)} %slice.113, bf16[512,8,16]{0,2,1:T(8,128)(2,1)} %get-tuple-element.108, bf16[512,8,16]{0,2,1:T(8,128)(2,1)} %get-tuple-element.109), kind=kOutput, calls=%fused_computation.43 | convolution fusion | flops 280498688 | bytes 18350080 | tf_op jit(solution)/shard_map/while/body/eval_jaxpr/hqk,khd->qhd/dot_general | solution.py:118
  144.7 13.9 %fusion.41 = f32[512,8,64]{0,2,1:T(8,128)} fusion(f32[8,512,512]{1,2,0:T(8,128)} %fusion.3, f32[8,512,512]{1,2,0:T(8,128)} %fusion.70, bf16[512,8,32]{0,2,1:T(8,128)(2,1)S(1)} %copy-done.17, bf16[512,8,16]{0,2,1:T(8,128)(2,1)} %get-tuple-element.101, bf16[512,8,16]{0,2,1:T(8,128)(2,1)} %get-tuple-element.100), kind=kOutput, calls=%fused_computation.44 | convolution fusion | flops 280498688 | bytes 18350080 | tf_op jit(solution)/shard_map/while/body/eval_jaxpr/hqk,qhd->khd/dot_general | solution.py:121
  168.1 6.1 fusion.83
  174.1 11.5 %fusion.82 = (f32[2048]{0:T(1024)S(1)}, bf16[512,2048]{1,0:T(8,128)(2,1)S(1)}) fusion(f32[512,2048]{1,0:T(8,128)} %fusion.83, f32[2048]{0:T(1024)S(1)} %copy-done.23, bf16[512,2048]{1,0:T(8,128)(2,1)S(1)} %copy-done.6, bf16[2048,2048]{1,0:T(8,128)(2,1)} %param.21), kind=kOutput, calls=%fused_computation.110 | convolution fusion | flops 4316985344 | bytes 16793600 | tf_op jit(solution)/shard_map/dot_general | solution.py:187
  186.9 7.7 convolution_add_fusion.2
  199.7 8.1 fusion.80
  212.6 8.6 fusion.29
  221.2 8.6 fusion.63
  229.8 8.9 fusion.79
  238.7 31.8 %reduce-scatter.8.cloned.1.call-done = f32[128,2048]{1,0:T(8,128)} async-done(((f32[512,2048]{1,0:T(8,128)}), f32[128,2048]{1,0:T(8,128)}) %reduce-scatter.8.cloned.1.call-update) | async-done | bytes 1048592 | tf_op jit(solution)/shard_map/reduce_scatter | solution.py:207
  283.7 66.2 %reduce-scatter.6.cloned.1.call-done = f32[128,2048]{1,0:T(8,128)} async-done(((f32[512,2048]{1,0:T(8,128)}), f32[128,2048]{1,0:T(8,128)}) %reduce-scatter.6.cloned.1.call-update) | async-done | bytes 1048592 | tf_op jit(solution)/shard_map/reduce_scatter | solution.py:175
  353.2 26.7 %reduce-scatter.10.cloned.1.call-done = f32[512,2]{1,0:T(8,128)} async-done(((f32[2048,2]{1,0:T(8,128)}), f32[512,2]{1,0:T(8,128)}) %reduce-scatter.10.cloned.1.call-update) | async-done | bytes 4112
  381.0 26.0 %all-reduce = (f32[2,512]{1,0:T(2,128)S(1)}, f32[3,512]{1,0:T(4,128)}, f32[2048]{0:T(1024)}, f32[2048]{0:T(1024)}) all-reduce(f32[2,512]{1,0:T(2,128)S(1)} %copy.59, f32[3,512]{1,0:T(4,128)S(1)} %reshape.220, f32[2048]{0:T(1024)S(1)} %get-tuple-element.114, ...), channel_id=1, replica_groups=mesh['replica'=8,'shard'=4] {'replica'}, use_global_device_ids=true, to_apply=%region_14.15 | all-reduce | flops 6656 | bytes 53248 | tf_op jit(solution)/shard_map/psum | solution.py:225
  407.6 555.2 %all-reduce.4.cloned.1.call-done = (f32[2048,3,512]{2,0,1:T(8,128)}, f32[512,2048]{1,0:T(8,128)}, f32[2048,2048]{1,0:T(8,128)}, f32[2048,2048]{1,0:T(8,128)}) async-done(((f32[2048,3,512]{2,0,1:T(8,128)}, f32[512,2048]{1,0:T(8,128)}, f32[2048,2048]{1,0:T(8,128)}, f32[2048,2048]{1,0:T(8,128)}), (f32[2048,3,512]{2,0,1:T(8,128)}, f32[512,2048]{1,0:T(8,128)}, f32[2048,2048]{1,0:T(8,128)}, ...) | async-done | bytes 50331664 | tf_op jit(solution)/shard_map/psum | solution.py:225
  962.8 11.1 %copy.64 = f32[2048,3,512]{2,0,1:T(8,128)} copy(f32[2048,3,512]{2,0,1:T(8,128)} %get-tuple-element.124) | data formatting | bytes 25165824
  976.0 14.0 %copy.66 = f32[2048,2048]{1,0:T(8,128)} copy(f32[2048,2048]{1,0:T(8,128)} %get-tuple-element.127) | data formatting | bytes 33554432
  992.0 6.3 copy.67
  (128 shorter events, 60.9 us)
Async XLA Ops:
  7.2 99.6 %copy-start = (bf16[512,2048]{1,0:T(8,128)(2,1)S(1)}, bf16[512,2048]{1,0:T(8,128)(2,1)}, u32[]{:S(2)}) copy-start(bf16[512,2048]{1,0:T(8,128)(2,1)} %param.18) | copy-start | bytes 6291460
  7.2 53.5 %all-gather.3.cloned.1.call-start = ((), (), s32[]{:S(2)}) async-start(), calls=%async_computation.3 | async-start | bytes 2621440 | tf_op jit(solution)/shard_map/all_gather | solution.py:162
  12.2 94.6 %all-gather.5.cloned.1.call-start = ((), (), s32[]{:S(2)}) async-start(), calls=%async_computation.5 | async-start | bytes 2621440 | tf_op jit(solution)/shard_map/all_gather | solution.py:183
  13.0 257.5 %reduce-scatter.8.cloned.1.call-start = ((), (), s32[]{:S(2)}) async-start(), calls=%async_computation.6 | async-start | bytes 5242880 | tf_op jit(solution)/shard_map/reduce_scatter | solution.py:207
  13.7 8.8 copy-start.20
  130.3 14.3 %copy-start.17 = (bf16[512,8,32]{0,2,1:T(8,128)(2,1)S(1)}, bf16[512,8,32]{0,2,1:T(8,128)(2,1)}, u32[]{:S(2)}) copy-start(bf16[512,8,32]{0,2,1:T(8,128)(2,1)} %slice.114) | copy-start | bytes 786436
  194.7 155.2 %reduce-scatter.6.cloned.1.call-start = ((), (), s32[]{:S(2)}) async-start(), calls=%async_computation.4 | async-start | bytes 5242880 | tf_op jit(solution)/shard_map/reduce_scatter | solution.py:175
  199.7 8.1 copy-start.8
  211.2 168.7 %reduce-scatter.10.cloned.1.call-start = ((), (), s32[]{:S(2)}) async-start(), calls=%async_computation.7 | async-start | bytes 1310720
  212.6 8.6 copy-start.22
  212.6 8.6 copy-start.25
  221.2 8.6 copy-start.7
  221.2 8.6 copy-start.27
  229.8 40.6 %copy-start.2 = (bf16[128,2048]{1,0:T(8,128)(2,1)S(1)}, bf16[128,2048]{1,0:T(8,128)(2,1)}, u32[]{:S(2)}) copy-start(bf16[128,2048]{1,0:T(8,128)(2,1)} %param.12) | copy-start | bytes 1572868
  229.8 40.6 %copy-start.18 = (f32[2048]{0:T(1024)S(1)}, f32[2048]{0:T(1024)}, u32[]{:S(2)}) copy-start(f32[2048]{0:T(1024)} %param.14) | copy-start | bytes 24580
  229.8 43.8 %copy-start.9 = (bf16[8,64,512]{2,1,0:T(8,128)(2,1)S(1)}, bf16[8,64,512]{2,1,0:T(8,128)(2,1)}, u32[]{:S(2)}) copy-start(bf16[8,64,512]{2,1,0:T(8,128)(2,1)} %copy-done.8) | copy-start | bytes 1572868
  273.6 689.2 %all-reduce.4.cloned.1.call-start = ((), (), s32[]{:S(2)}) async-start(), calls=%async_computation.8 | async-start | bytes 100663296 | tf_op jit(solution)/shard_map/psum | solution.py:225
  280.1 69.9 %copy-start.14 = (bf16[128,2048]{1,0:T(8,128)(2,1)S(1)}, bf16[128,2048]{1,0:T(8,128)(2,1)}, u32[]{:S(2)}) copy-start(bf16[128,2048]{1,0:T(8,128)(2,1)} %param.23) | copy-start | bytes 1572868
  280.1 69.9 %copy-start.19 = (f32[2048]{0:T(1024)S(1)}, f32[2048]{0:T(1024)}, u32[]{:S(2)}) copy-start(f32[2048]{0:T(1024)} %param.22) | copy-start | bytes 24580
  962.8 11.1 %copy-start.10 = (f32[512,2048]{1,0:T(8,128)S(1)}, f32[512,2048]{1,0:T(8,128)}, u32[]{:S(2)}) copy-start(f32[512,2048]{1,0:T(8,128)} %get-tuple-element.126) | copy-start | bytes 12582916
  973.8 16.2 %slice-start = ((s8[16777216]{0:T(1024)(128)(4,1)}), s8[4194304]{0:T(1024)(128)(4,1)S(1)}, s32[]{:S(2)}) async-start(s8[16777216]{0:T(1024)(128)(4,1)} %bitcast.69), calls=%async_computation.9 | async-start | bytes 8388608
  976.0 14.0 %slice-start.1 = ((s8[16777216]{0:T(1024)(128)(4,1)}), s8[4194304]{0:T(1024)(128)(4,1)S(1)}, s32[]{:S(2)}) async-start(s8[16777216]{0:T(1024)(128)(4,1)} %bitcast.69), calls=%async_computation.10 | async-start | bytes 8388608
  976.0 14.0 %slice-start.2 = ((s8[16777216]{0:T(1024)(128)(4,1)}), s8[4194304]{0:T(1024)(128)(4,1)S(1)}, s32[]{:S(2)}) async-start(s8[16777216]{0:T(1024)(128)(4,1)} %bitcast.69), calls=%async_computation.11 | async-start | bytes 8388608
  976.0 16.0 %slice-start.3 = ((s8[16777216]{0:T(1024)(128)(4,1)}), s8[4194304]{0:T(1024)(128)(4,1)S(1)}, s32[]{:S(2)}) async-start(s8[16777216]{0:T(1024)(128)(4,1)} %bitcast.69), calls=%async_computation.12 | async-start | bytes 8388608
  (20 other events, 75.6 us)
Sparse Core Ops, SparseCore 0:
  12.3 48.3 all-gather.2
  62.3 44.4 all-gather.4
  194.8 75.5 reduce-scatter.7
  272.6 77.2 reduce-scatter.5
  352.1 27.8 reduce-scatter.9
  385.2 577.5 all-reduce.3
where the time goes:
time: 1010 us
  waiting for transfers between devices  749 us (74%)
  matrix products  136 us (13%)
  local copies, waits for them, and re-layouts  62.2 us (6%)
  blocking collectives  26 us (3%)
  other arithmetic  17.1 us (2%)
  between operations  15 us (1%)
    psum x1, waiting for transfers between devices, shards(): lax.psum((grad_qkv_w, grad_qkv_b, grad_out_w, grad_fc1, grad_fc1_b, grad_...  555 us
    reduce_scatter x1, waiting for transfers between devices, shards(): lax.psum_scatter(jnp.dot(context_flat, out_weight, preferred_element_type...  66.2 us
    unnamed x79, local copies, waits for them, and re-layouts  53.9 us
    all_gather x1, waiting for transfers between devices, shards(): normed_full = lax.all_gather(normed, 'shard', axis=0, tiled=True)  37.5 us
    reduce_scatter x1, waiting for transfers between devices, shards(): lax.psum_scatter(jnp.dot(grad_qkv_low, qkv_flat.T, preferred_element_type...  31.8 us
    all_gather x1, waiting for transfers between devices, shards(): cot_full = lax.all_gather(cotangent, 'shard', axis=0, tiled=True)  30.3 us
    unnamed x7, waiting for transfers between devices  27.5 us
    psum x1, blocking collectives, shards(): lax.psum((grad_qkv_w, grad_qkv_b, grad_out_w, grad_fc1, grad_fc1_b, grad_...  26 us
  transfers between devices with their start and end apart: 6, of which 6 were waited for; matrix products, arithmetic and copies ran while one was open for 8% of the time, Pallas kernels for 0%

commit v1 on v0

--- a/solution.py
+++ b/solution.py
@@ -221,21 +221,14 @@
         - jnp.mean(scaled, axis=-1, keepdims=True)
         - x_hat * jnp.mean(scaled * x_hat, axis=-1, keepdims=True)
     )
-    grad_qkv_w, grad_qkv_b, grad_out_w, grad_fc1, grad_fc1_b, grad_fc2, grad_out_b, norm_shares = (
-        lax.psum(
-            (
-                grad_qkv_w,
-                grad_qkv_b,
-                grad_out_w,
-                grad_fc1,
-                grad_fc1_b,
-                grad_fc2,
-                grad_out_b,
-                norm_shares,
-            ),
-            "replica",
-        )
-    )
+    grad_qkv_b, grad_fc1_b, grad_out_b, norm_shares = lax.psum(
+        (grad_qkv_b, grad_fc1_b, grad_out_b, norm_shares), "replica"
+    )
+    low_sums = lax.psum(
+        tuple(g.astype(jnp.bfloat16) for g in (grad_qkv_w, grad_out_w, grad_fc1, grad_fc2)),
+        "replica",
+    )
+    grad_qkv_w, grad_out_w, grad_fc1, grad_fc2 = (g.astype(jnp.float32) for g in low_sums)
     return (
         output,
         input_grad,

time: 1010 us -> 741 us (0.73)
  waiting for transfers between devices: 749 us -> 482 us
  local copies, waits for them, and re-layouts: 62.2 us -> 22.7 us
  other arithmetic: 17.1 us -> 52.6 us
    psum x1, waiting for transfers between devices: 555 us -> 283 us  [shards(): lax.psum(tuple((g.astype(jnp.bfloat16) for g in (grad_qkv_w, grad_out_w,...]
    unnamed x79 -> x59, local copies, waits for them, and re-layouts: 53.9 us -> 14.4 us
    convert_element_type x0 -> x4, other arithmetic: none -> 34.2 us  [shards(): g.astype(jnp.float32)]
  transfers between devices with their start and end apart: 6 -> 6, of which waited for: 6 -> 6; matrix products, arithmetic and copies ran while one was open for 8% -> 11% of each run, Pallas kernels for 0% -> 0%
where the time goes in v1:
time: 741 us; the launch traced here: 733 us
  waiting for transfers between devices  482 us (65%)
  matrix products  134 us (18%)
  other arithmetic  52.6 us (7%)
  blocking collectives  26 us (4%)
  local copies, waits for them, and re-layouts  22.7 us (3%)
  between operations  15 us (2%)
    psum x1, waiting for transfers between devices, shards(): lax.psum(tuple((g.astype(jnp.bfloat16) for g in (grad_qkv_w, grad_out_w,...  283 us
    reduce_scatter x1, waiting for transfers between devices, shards(): lax.psum_scatter(jnp.dot(context_flat, out_weight, preferred_element_type...  67.2 us
    all_gather x1, waiting for transfers between devices, shards(): normed_full = lax.all_gather(normed, 'shard', axis=0, tiled=True)  37.5 us
    reduce_scatter x1, waiting for transfers between devices, shards(): lax.psum_scatter(jnp.dot(grad_qkv_low, qkv_flat.T, preferred_element_type...  36.1 us
    convert_element_type x4, other arithmetic, shards(): g.astype(jnp.float32)  34.2 us
    all_gather x1, waiting for transfers between devices, shards(): cot_full = lax.all_gather(cotangent, 'shard', axis=0, tiled=True)  30.3 us
    unnamed x7, waiting for transfers between devices  27.5 us
    psum x1, blocking collectives, shards(): lax.psum((grad_qkv_b, grad_fc1_b, grad_out_b, norm_shares), 'replica')  26 us
  transfers between devices with their start and end apart: 6, of which 6 were waited for; matrix products, arithmetic and copies ran while one was open for 11% of the time, Pallas kernels for 0%

profile of v1, /device:TPU:0, one launch (start us, length us, event | category | flops | bytes accessed | tf_op | source)
XLA Modules:
  0.0 732.9 jit_solution(2110832071851290796)
XLA Ops:
  13.7 8.8 %copy.45 = bf16[2048,3,512]{0,2,1:T(8,128)(2,1)} copy(bf16[2048,3,512]{2,0,1:T(8,128)(2,1)} %param.16) | data formatting | bytes 12582912 | tf_op args[4]
  23.2 37.5 %all-gather.3.cloned.1.call-done = bf16[512,2048]{1,0:T(8,128)(2,1)} async-done(((bf16[128,2048]{1,0:T(8,128)(2,1)}), bf16[512,2048]{1,0:T(8,128)(2,1)}) %all-gather.3.cloned.1.call-update) | async-done | bytes 2097168 | tf_op jit(solution)/shard_map/all_gather | solution.py:162
  60.7 8.5 %convolution_add_fusion.1 = f32[512,1536]{1,0:T(8,128)} fusion(bf16[512,2048]{1,0:T(8,128)(2,1)} %all-gather.3.cloned.1.call-done, bf16[2048,1536]{0,1:T(8,128)(2,1)} %bitcast.69, f32[1536]{0:T(1024)S(1)} %add.117), kind=kOutput, calls=%fused_computation.31 | convolution fusion | flops 3222011904 | bytes 11540480 | tf_op jit(solution)/shard_map/dot_general | solution.py:163
  76.5 30.3 %all-gather.5.cloned.1.call-done = bf16[512,2048]{1,0:T(8,128)(2,1)} async-done(((bf16[128,2048]{1,0:T(8,128)(2,1)}), bf16[512,2048]{1,0:T(8,128)(2,1)}) %all-gather.5.cloned.1.call-update) | async-done | bytes 2097168 | tf_op jit(solution)/shard_map/all_gather | solution.py:183
  109.7 6.1 fusion.68
  116.8 8.7 %fusion.3 = f32[8,512,512]{1,2,0:T(8,128)} fusion(pred[512,512]{0,1:T(8,128)(4,1)S(1)} %fusion.64, bf16[512,8,32]{0,2,1:T(8,128)(2,1)} %slice.113, bf16[512,8,16]{0,2,1:T(8,128)(2,1)} %get-tuple-element.108, bf16[512,8,16]{0,2,1:T(8,128)(2,1)} %get-tuple-element.109, bf16[512,8,32]{0,2,1:T(8,128)(2,1)} %slice.114, ...), kind=kOutput, calls=%fused_computation.4 | convolution fusion | flops 553652736 | bytes 9699328 | tf_op jit(solution)/shard_map/while/body/eval_jaxpr/reduce_sum | solution.py:82
  125.5 5.0 fusion.34
  130.5 14.6 %fusion.37 = f32[512,8,64]{0,2,1:T(8,128)} fusion(f32[8,512,512]{1,2,0:T(8,128)} %fusion.3, f32[8,512,512]{1,2,0:T(8,128)} %fusion.68, bf16[512,8,32]{0,2,1:T(8,128)(2,1)} %slice.113, bf16[512,8,16]{0,2,1:T(8,128)(2,1)} %get-tuple-element.108, bf16[512,8,16]{0,2,1:T(8,128)(2,1)} %get-tuple-element.109), kind=kOutput, calls=%fused_computation.46 | convolution fusion | flops 280498688 | bytes 18350080 | tf_op jit(solution)/shard_map/while/body/eval_jaxpr/hqk,khd->qhd/dot_general | solution.py:118
  145.1 13.9 %fusion.40 = f32[512,8,64]{0,2,1:T(8,128)} fusion(f32[8,512,512]{1,2,0:T(8,128)} %fusion.3, f32[8,512,512]{1,2,0:T(8,128)} %fusion.68, bf16[512,8,32]{0,2,1:T(8,128)(2,1)S(1)} %copy-done.13, bf16[512,8,16]{0,2,1:T(8,128)(2,1)} %get-tuple-element.101, bf16[512,8,16]{0,2,1:T(8,128)(2,1)} %get-tuple-element.100), kind=kOutput, calls=%fused_computation.47 | convolution fusion | flops 280498688 | bytes 18350080 | tf_op jit(solution)/shard_map/while/body/eval_jaxpr/hqk,qhd->khd/dot_general | solution.py:121
  168.8 6.1 fusion.80
  174.9 12.6 %fusion.79 = (f32[2048]{0:T(1024)S(1)}, bf16[512,2048]{1,0:T(8,128)(2,1)}) fusion(f32[512,2048]{1,0:T(8,128)} %fusion.80, f32[2048]{0:T(1024)S(1)} %copy-done.19, bf16[512,2048]{1,0:T(8,128)(2,1)S(1)} %copy-done.10, bf16[2048,2048]{1,0:T(8,128)(2,1)} %param.21), kind=kOutput, calls=%fused_computation.111 | convolution fusion | flops 4316985344 | bytes 16793600 | tf_op jit(solution)/shard_map/dot_general | solution.py:187
  187.5 7.7 %convolution_add_fusion.2 = f32[512,2048]{1,0:T(8,128)} fusion(f32[512,2048]{1,0:T(8,128)S(1)} %copy-done.20, bf16[2048,2048]{1,0:T(8,128)(2,1)S(1)} %bitcast.89, bf16[512,2048]{1,0:T(8,128)(2,1)} %get-tuple-element.115), kind=kOutput, calls=%fused_computation.33 | convolution fusion | flops 4296015872 | bytes 18874368 | tf_op jit(solution)/shard_map/dot_general | solution.py:209
  200.2 8.0 %fusion.77 = f32[512,2048]{1,0:T(8,128)S(1)} fusion(bf16[2048,2048]{1,0:T(8,128)(2,1)} %param.21, f32[512,2048]{1,0:T(8,128)S(1)} %copy-done.21, f32[2048]{0:T(1024)S(1)} %copy-done.19), kind=kOutput, calls=%fused_computation.109 | convolution fusion | flops 4305453056 | bytes 16785408 | tf_op jit(solution)/shard_map/dot_general | solution.py:177
  212.0 8.4 %convolution_convert_fusion.2 = bf16[2048,3,512]{2,0,1:T(8,128)(2,1)} fusion(bf16[3,512,512]{2,1,0:T(8,128)(2,1)} %bitcast.79, bf16[512,2048]{1,0:T(8,128)(2,1)} %all-gather.3.cloned.1.call-done), kind=kOutput, calls=%fused_computation.16 | convolution fusion | flops 3224371200 | bytes 9961472 | tf_op jit(solution)/shard_map/dot_general | solution.py:204
  220.4 6.8 convolution_convert_fusion.1
  227.2 7.6 %convolution_convert_fusion = bf16[2048,2048]{1,0:T(8,128)(2,1)} fusion(bf16[512,2048]{1,0:T(8,128)(2,1)S(1)} %copy-done.11, f32[512,2048]{1,0:T(8,128)S(1)} %copy-done.22, f32[2048]{0:T(1024)S(1)} %copy-done.19), kind=kOutput, calls=%fused_computation.11 | convolution fusion | flops 4309647360 | bytes 14688256 | tf_op jit(solution)/shard_map/dot_general | solution.py:185
  234.8 36.1 %reduce-scatter.8.cloned.1.call-done = f32[128,2048]{1,0:T(8,128)} async-done(((f32[512,2048]{1,0:T(8,128)}), f32[128,2048]{1,0:T(8,128)}) %reduce-scatter.8.cloned.1.call-update) | async-done | bytes 1048592 | tf_op jit(solution)/shard_map/reduce_scatter | solution.py:207
  283.2 67.2 %reduce-scatter.6.cloned.1.call-done = f32[128,2048]{1,0:T(8,128)} async-done(((f32[512,2048]{1,0:T(8,128)}), f32[128,2048]{1,0:T(8,128)}) %reduce-scatter.6.cloned.1.call-update) | async-done | bytes 1048592 | tf_op jit(solution)/shard_map/reduce_scatter | solution.py:175
  353.7 26.7 %reduce-scatter.10.cloned.1.call-done = f32[512,2]{1,0:T(8,128)} async-done(((f32[2048,2]{1,0:T(8,128)}), f32[512,2]{1,0:T(8,128)}) %reduce-scatter.10.cloned.1.call-update) | async-done | bytes 4112
  381.5 26.0 %all-reduce = (f32[2,512]{1,0:T(2,128)S(1)}, f32[3,512]{1,0:T(4,128)}, f32[2048]{0:T(1024)}, f32[2048]{0:T(1024)}) all-reduce(f32[2,512]{1,0:T(2,128)S(1)} %copy.59, f32[3,512]{1,0:T(4,128)S(1)} %reshape.220, f32[2048]{0:T(1024)S(1)} %get-tuple-element.114, ...), channel_id=1, replica_groups=mesh['replica'=8,'shard'=4] {'replica'}, use_global_device_ids=true, to_apply=%region_14.15 | all-reduce | flops 6656 | bytes 53248 | tf_op jit(solution)/shard_map/psum | solution.py:224
  408.1 283.2 %all-reduce.4.cloned.1.call-done = (bf16[2048,3,512]{2,0,1:T(8,128)(2,1)}, bf16[512,2048]{1,0:T(8,128)(2,1)}, bf16[2048,2048]{1,0:T(8,128)(2,1)}, bf16[2048,2048]{1,0:T(8,128)(2,1)}) async-done(((bf16[2048,3,512]{2,0,1:T(8,128)(2,1)}, bf16[512,2048]{1,0:T(8,128)(2,1)}, bf16[2048,2048]{1,0:T(8,128)(2,1)}, bf16[2048,2048]{1,0:T(8,128)(2,1)}), (bf16[2048,3,512]{2,0,1:T(8,128)(2,1)}, ...) | async-done | bytes 25165840 | tf_op jit(solution)/shard_map/psum | solution.py:227
  695.6 6.6 convert_element_type.111
  702.2 11.7 %convert_element_type.115 = f32[2048,2048]{1,0:T(8,128)} convert(bf16[2048,2048]{1,0:T(8,128)(2,1)} %get-tuple-element.92) | non-fusion elementwise | flops 4194304 | bytes 25165824 | tf_op jit(solution)/shard_map/convert_element_type | solution.py:231
  713.9 11.7 %convert_element_type.117 = f32[2048,2048]{1,0:T(8,128)} convert(bf16[2048,2048]{1,0:T(8,128)(2,1)} %get-tuple-element.93) | non-fusion elementwise | flops 4194304 | bytes 25165824 | tf_op jit(solution)/shard_map/convert_element_type | solution.py:231
  (111 shorter events, 58.0 us)
Async XLA Ops:
  7.2 99.6 %copy-start = (bf16[512,2048]{1,0:T(8,128)(2,1)S(1)}, bf16[512,2048]{1,0:T(8,128)(2,1)}, u32[]{:S(2)}) copy-start(bf16[512,2048]{1,0:T(8,128)(2,1)} %param.18) | copy-start | bytes 6291460
  7.2 53.5 %all-gather.3.cloned.1.call-start = ((), (), s32[]{:S(2)}) async-start(), calls=%async_computation.3 | async-start | bytes 2621440 | tf_op jit(solution)/shard_map/all_gather | solution.py:162
  12.2 94.6 %all-gather.5.cloned.1.call-start = ((), (), s32[]{:S(2)}) async-start(), calls=%async_computation.5 | async-start | bytes 2621440 | tf_op jit(solution)/shard_map/all_gather | solution.py:183
  13.0 258.0 %reduce-scatter.8.cloned.1.call-start = ((), (), s32[]{:S(2)}) async-start(), calls=%async_computation.6 | async-start | bytes 5242880 | tf_op jit(solution)/shard_map/reduce_scatter | solution.py:207
  13.7 8.8 %copy-start.16 = (s32[1,8]{1,0:T(1,128)S(1)}, s32[1,8]{1,0:T(1,128)}, u32[]{:S(2)}) copy-start(s32[1,8]{1,0:T(1,128)} %param.13) | copy-start | bytes 100
  109.7 6.1 copy-start.8
  109.7 6.1 copy-start.7
  130.5 30.3 %copy-start.2 = (f32[512,1,8,64]{0,3,2,1:T(8,128)}, f32[512,1,8,64]{0,3,2,1:T(8,128)S(1)}, u32[]{:S(2)}) copy-start(f32[512,1,8,64]{0,3,2,1:T(8,128)S(1)} %fusion.34) | copy-start | bytes 3145732
  130.5 14.7 %copy-start.13 = (bf16[512,8,32]{0,2,1:T(8,128)(2,1)S(1)}, bf16[512,8,32]{0,2,1:T(8,128)(2,1)}, u32[]{:S(2)}) copy-start(bf16[512,8,32]{0,2,1:T(8,128)(2,1)} %slice.114) | copy-start | bytes 786436
  160.8 7.9 %slice-start.4 = ((s8[8388608]{0:T(1024)(128)(4,1)}), s8[4194304]{0:T(1024)(128)(4,1)S(1)}, s32[]{:S(2)}) async-start(s8[8388608]{0:T(1024)(128)(4,1)} %bitcast.88), calls=%async_computation.13 | async-start | bytes 8388608
  162.1 6.6 copy-start.12
  168.8 6.1 copy-start.10
  174.9 12.6 %copy-start.20 = (f32[512,2048]{1,0:T(8,128)S(1)}, f32[512,2048]{1,0:T(8,128)}, u32[]{:S(2)}) copy-start(f32[512,2048]{1,0:T(8,128)} %fusion.81) | copy-start | bytes 12582916
  195.2 155.2 %reduce-scatter.6.cloned.1.call-start = ((), (), s32[]{:S(2)}) async-start(), calls=%async_computation.4 | async-start | bytes 5242880 | tf_op jit(solution)/shard_map/reduce_scatter | solution.py:175
  211.6 168.8 %reduce-scatter.10.cloned.1.call-start = ((), (), s32[]{:S(2)}) async-start(), calls=%async_computation.7 | async-start | bytes 1310720
  211.9 8.4 %copy-start.18 = (bf16[512,2048]{1,0:T(8,128)(2,1)S(1)}, bf16[512,2048]{1,0:T(8,128)(2,1)}, u32[]{:S(2)}) copy-start(bf16[512,2048]{1,0:T(8,128)(2,1)} %all-gather.3.cloned.1.call-done) | copy-start | bytes 6291460
  211.9 8.4 %copy-start.23 = (bf16[512,2048]{1,0:T(8,128)(2,1)S(1)}, bf16[512,2048]{1,0:T(8,128)(2,1)}, u32[]{:S(2)}) copy-start(bf16[512,2048]{1,0:T(8,128)(2,1)} %get-tuple-element.115) | copy-start | bytes 6291460
  220.4 6.9 copy-start.11
  220.4 6.9 copy-start.22
  227.2 43.7 %copy-start.1 = (bf16[128,2048]{1,0:T(8,128)(2,1)S(1)}, bf16[128,2048]{1,0:T(8,128)(2,1)}, u32[]{:S(2)}) copy-start(bf16[128,2048]{1,0:T(8,128)(2,1)} %param.12) | copy-start | bytes 1572868
  227.2 43.7 %copy-start.14 = (f32[2048]{0:T(1024)S(1)}, f32[2048]{0:T(1024)}, u32[]{:S(2)}) copy-start(f32[2048]{0:T(1024)} %param.14) | copy-start | bytes 24580
  274.0 417.3 %all-reduce.4.cloned.1.call-start = ((), (), s32[]{:S(2)}) async-start(), calls=%async_computation.8 | async-start | bytes 50331648 | tf_op jit(solution)/shard_map/psum | solution.py:227
  278.3 72.2 %copy-start.9 = (bf16[128,2048]{1,0:T(8,128)(2,1)S(1)}, bf16[128,2048]{1,0:T(8,128)(2,1)}, u32[]{:S(2)}) copy-start(bf16[128,2048]{1,0:T(8,128)(2,1)} %param.23) | copy-start | bytes 1572868
  278.3 72.1 %copy-start.15 = (f32[2048]{0:T(1024)S(1)}, f32[2048]{0:T(1024)}, u32[]{:S(2)}) copy-start(f32[2048]{0:T(1024)} %param.22) | copy-start | bytes 24580
  (12 other events, 38.0 us)
Sparse Core Ops, SparseCore 0:
  12.3 48.3 all-gather.2
  62.3 44.4 all-gather.4
  195.3 75.5 reduce-scatter.7
  273.1 77.2 reduce-scatter.5
  352.6 27.7 reduce-scatter.9
  385.6 305.6 all-reduce.3
